TPU v7x, 32 devices: a whole 2x2x4 slice. The times are simulated.
32 devices in a mesh: layer: 2 (over core), tok: 16 (over z, y, x).
Axes of the slice: x: 2, y: 2, z: 4, core: 2. Of those that a mesh axis runs over, the one named last changes fastest.
Arguments:
- train_act: bfloat16 [4, 32768, 256], P('layer', 'tok'), may hold values from -0.75 to 0.75
- train_grad: bfloat16 [4, 32768, 256], P('layer', 'tok'), may hold values from -0.75 to 0.75
- test_act: bfloat16 [4, 2048, 256], P('layer', 'tok'), may hold values from -0.75 to 0.75
- test_grad: bfloat16 [4, 2048, 256], P('layer', 'tok'), may hold values from -0.75 to 0.75
- segment_ids: int32 [2048], replicated, may hold values from 0 to 127, as said below
Outputs:
- scores: float32 [128, 32768], P('layer', 'tok')
Inputs may be any that keep to these rules, and one draw needn't show every extreme that they name: `segment_ids`: each of the 128 queries has exactly 16 test tokens, placed anywhere among the 2048.
All inputs are finite; a program needn't handle non-finite values.
Results may differ from a plain program's by a relative error of at most 0.0029.
Values may be sent and summed in bfloat16 or wider, within the bound.
A program may use at most 128 MiB of HBM per device.

v0:
```python
import functools
import math

import jax
import jax.numpy as jnp
from jax import lax
from jax.experimental import pallas as pl
from jax.experimental.pallas import tpu as pltpu
from jax.sharding import PartitionSpec as P

Q = 128
MESH = pl.DeviceIdType.MESH


def kernel(
    layers,
    line,
    train_a,
    train_g,
    test_a,
    test_g,
    ids_ref,
    out_ref,
    ta,
    tg,
    buf,
    acc,
    xbuf,
    train_sem,
    own_sem,
    recv_sem,
    send_sem,
    xs_sem,
    xr_sem,
):
    me = lax.axis_index("tok")
    core = lax.axis_index("layer")
    z = me // 4
    y = (me // 2) % 2
    x = me % 2
    own_col = y * 2 + x
    x_col = y * 2 + (1 - x)
    y_col = (1 - y) * 2 + x
    d_col = (1 - y) * 2 + (1 - x)
    x_dev = z * 4 + x_col
    y_dev = z * 4 + y_col
    has_up = z < line - 1
    has_down = z > 0
    layer_count, train_rows, _ = ta.shape
    rows = buf.shape[3]
    q_block = Q // layers

    for which, (src, dst) in enumerate(((train_a, ta), (train_g, tg))):
        pltpu.make_async_copy(src, dst, train_sem.at[which]).start()
    for which, src in enumerate((test_a, test_g)):
        pltpu.make_async_copy(src, buf.at[which, :, z * 4], own_sem.at[which]).start()

    barrier = pltpu.get_barrier_semaphore()

    def greet(where):
        pl.semaphore_signal(barrier, inc=1, device_id=where, device_id_type=MESH)

    greet({"tok": x_dev})
    greet({"tok": y_dev})
    pl.when(has_up)(lambda: greet({"tok": me + 4}))
    pl.when(has_down)(lambda: greet({"tok": me - 4}))
    for step in range(1, layers):
        greet({"layer": lax.rem(core + step, layers)})
    ends = jnp.where(has_up, 1, 0) + jnp.where(has_down, 1, 0)
    pl.semaphore_wait(barrier, layers + 1 + ends)

    def copy(route, which, zz, held, there, to, src=None):
        return pltpu.make_async_remote_copy(
            src_ref=buf.at[which, :, zz * 4 + held] if src is None else src,
            dst_ref=buf.at[which, :, zz * 4 + there],
            send_sem=send_sem.at[route, which, zz],
            recv_sem=recv_sem.at[which, zz * 4 + there],
            device_id={"tok": to},
            device_id_type=MESH,
        )

    def arrived(which, zz, there):
        copy(0, which, zz, 0, there, x_dev).wait_recv()

    def nth(i):
        low = z < line - 1 - z
        near = jnp.where(low, z, line - 1 - z)
        half = (i + 1) // 2
        side = jnp.where(i % 2 == 1, z - half, z + half)
        rest = jnp.where(low, i, line - 1 - i)
        return jnp.where(i <= 2 * near, side, rest)

    for which, src in enumerate((test_a, test_g)):
        pl.when(has_up)(lambda: copy(3, which, z, 0, 0, me + 4, src).start())
        pl.when(has_down)(lambda: copy(4, which, z, 0, 0, me - 4, src).start())
        copy(0, which, z, 0, 2, x_dev, src).start()
        copy(1, which, z, 0, 3, y_dev, src).start()

    acc[...] = jnp.zeros_like(acc)
    _, tiles, _, tile = xbuf.shape
    labels = lax.broadcasted_iota(jnp.int32, (Q, rows), 0)
    nt = (((1,), (1,)), ((), ()))

    def exchange(step, j):
        to = lax.rem(core + step, layers)
        theirs = pl.ds(pl.multiple_of(to * q_block, q_block), q_block)
        return pltpu.make_async_remote_copy(
            src_ref=acc.at[theirs, pl.ds(pl.multiple_of(j * tile, tile), tile)],
            dst_ref=xbuf.at[step - 1, j],
            send_sem=xs_sem.at[step - 1, j],
            recv_sem=xr_sem.at[step - 1, j],
            device_id={"layer": to},
            device_id_type=MESH,
        )

    def accumulate(zz, first, columns, final=None):
        one_hot = [
            jnp.where(ids_ref[zz * 4 + c] == labels, 1.0, 0.0).astype(jnp.bfloat16)
            for c in columns
        ]
        select = jnp.concatenate(one_hot * layer_count, axis=1)
        pair = pl.ds(zz * 4 + first, 2)

        def held(which, layer):
            return buf[which, layer, pair].reshape(2 * rows, buf.shape[4])

        def one_tile(j, carry):
            at = pl.ds(pl.multiple_of(j * tile, tile), tile)
            products = []
            for layer in range(layer_count):
                a_gram = lax.dot_general(
                    held(0, layer), ta[layer, at, :], nt, preferred_element_type=jnp.float32
                )
                g_gram = lax.dot_general(
                    held(1, layer), tg[layer, at, :], nt, preferred_element_type=jnp.float32
                )
                products.append((a_gram * g_gram).astype(jnp.bfloat16))
            acc[:, at] += jnp.dot(
                select, jnp.concatenate(products, axis=0), preferred_element_type=jnp.float32
            )
            if final is not None:

                @pl.when(final)
                def _():
                    for step in range(1, layers):
                        exchange(step, j).start()

            return carry

        lax.fori_loop(0, tiles, one_tile, 0)

    for which, (src, dst) in enumerate(((train_a, ta), (train_g, tg))):
        pltpu.make_async_copy(src, dst, train_sem.at[which]).wait()
    for which, src in enumerate((test_a, test_g)):
        pltpu.make_async_copy(src, buf.at[which, :, z * 4], own_sem.at[which]).wait()

    def stage(i, carry):
        zi = nth(i)

        @pl.when(i + 1 < line)
        def _():
            zn = nth(i + 1)
            for which in range(2):
                arrived(which, zn, 0)
                pl.when((zn < z) & has_up)(lambda: copy(3, which, zn, 0, 0, me + 4).start())
                pl.when((zn > z) & has_down)(lambda: copy(4, which, zn, 0, 0, me - 4).start())
                copy(0, which, zn, 0, 2, x_dev).start()
                copy(1, which, zn, 0, 3, y_dev).start()

        @pl.when(i < line)
        def _():
            arrived(0, zi, 2)
            copy(2, 0, zi, 2, 1, y_dev).start()
            arrived(0, zi, 3)
            arrived(1, zi, 3)
            copy(2, 1, zi, 3, 1, x_dev).start()
            arrived(1, zi, 2)
            accumulate(zi, 2, (x_col, y_col))

        @pl.when(i > 0)
        def _():
            zd = nth(i - 1)
            for which in range(2):
                arrived(which, zd, 1)
            accumulate(zd, 0, (own_col, d_col), i == line)

        return carry

    lax.fori_loop(0, line + 1, stage, 0)

    def drain(zz, carry):
        for which in range(2):
            copy(0, which, zz, 0, 2, x_dev).wait_send()
            copy(1, which, zz, 0, 3, y_dev).wait_send()
            copy(2, which, zz, 2, 1, y_dev).wait_send()
            pl.when((zz <= z) & has_up)(lambda: copy(3, which, zz, 0, 0, me + 4).wait_send())
            pl.when((zz >= z) & has_down)(lambda: copy(4, which, zz, 0, 0, me - 4).wait_send())
        return carry

    lax.fori_loop(0, line, drain, 0)

    mine = pl.ds(pl.multiple_of(core * q_block, q_block), q_block)
    for j in range(tiles):
        at = pl.ds(j * tile, tile)
        for step in range(1, layers):
            exchange(step, j).wait_recv()
        result = acc[mine, at]
        for step in range(1, layers):
            result = result + xbuf[step - 1, j]
        out_ref[:, at] = result
    for j in range(tiles):
        for step in range(1, layers):
            exchange(step, j).wait_send()


def on_device(layers, toks, train_act, train_grad, test_act, test_grad, segment_ids):
    layer_count, train_rows, width = train_act.shape
    rows = test_act.shape[1]
    line = toks // 4
    tile = math.gcd(train_rows, 1024)
    tiles = train_rows // tile
    q_block = Q // layers
    ids = segment_ids.reshape(toks, 1, rows)
    dma = pltpu.SemaphoreType.DMA
    anywhere = pl.BlockSpec(memory_space=pl.ANY)
    return pl.pallas_call(
        functools.partial(kernel, layers, line),
        out_shape=jax.ShapeDtypeStruct((q_block, train_rows), jnp.float32),
        in_specs=[anywhere] * 4 + [pl.BlockSpec(memory_space=pltpu.VMEM)],
        out_specs=pl.BlockSpec(memory_space=pltpu.VMEM),
        scratch_shapes=[
            pltpu.VMEM((layer_count, train_rows, width), jnp.bfloat16),
            pltpu.VMEM((layer_count, train_rows, width), jnp.bfloat16),
            pltpu.VMEM((2, layer_count, toks, rows, width), jnp.bfloat16),
            pltpu.VMEM((Q, train_rows), jnp.float32),
            pltpu.VMEM((layers - 1, tiles, q_block, tile), jnp.float32),
            dma((2,)),
            dma((2,)),
            dma((2, toks)),
            dma((5, 2, line)),
            dma((layers - 1, tiles)),
            dma((layers - 1, tiles)),
        ],
        compiler_params=pltpu.CompilerParams(
            collective_id=0, has_side_effects=True, vmem_limit_bytes=63 * 1024 * 1024
        ),
    )(train_act, train_grad, test_act, test_grad, ids)


def solution(mesh):
    placed = (
        P("layer", "tok", None),
        P("layer", "tok", None),
        P("layer", "tok", None),
        P("layer", "tok", None),
        P(),
    )
    body = functools.partial(on_device, mesh.shape["layer"], mesh.shape["tok"])
    return jax.shard_map(
        body, mesh=mesh, in_specs=placed, out_specs=P("layer", "tok"), check_vma=False
    )
```

profile of v0, /device:TPU:0, one launch (start us, length us, event | category | flops | bytes accessed | tf_op | source)
XLA Modules:
  0.0 46.5 jit_solution(2718740003350540472)
XLA Ops:
  0.0 44.7 %shard_map.55 = f32[64,2048]{1,0:T(8,128)} custom-call(bf16[2,2048,256]{2,1,0:T(8,128)(2,1)} %train_a.1, bf16[2,2048,256]{2,1,0:T(8,128)(2,1)} %train_g.1, bf16[2,128,256]{2,1,0:T(8,128)(2,1)} %test_a.1, bf16[2,128,256]{2,1,0:T(8,128)(2,1)} %test_g.1, s32[16,1,128]{2,1,0:T(1,128)} %bitcast.1), custom_call_target="tpu_custom_call" | custom-call | tf_op jit(solution)/shard_map/pallas_call | solution.py:226
  44.7 1.9 %copy.7 = f32[64,2048]{1,0:T(8,128)} copy(f32[64,2048]{1,0:T(8,128)} %shard_map.55) | data formatting | bytes 1048576
where the time goes:
time: 46.7 us; the launch traced here: 46.5 us
  Pallas kernels  44.7 us (96%)
  local copies, waits for them, and re-layouts  1.87 us (4%)
    pallas_call x1, Pallas kernels, on_device(): pl.pallas_call(functools.partial(kernel, layers, line), out_shape=jax.Sha...  44.7 us
    unnamed x1, local copies, waits for them, and re-layouts  1.87 us

commit v1 on v0

v1 whole, which is shorter than its diff:
```python
import functools
import heapq
import math

import jax
import jax.numpy as jnp
from jax import lax
from jax.experimental import pallas as pl
from jax.experimental.pallas import tpu as pltpu
from jax.sharding import PartitionSpec as P

Q = 128
MESH = pl.DeviceIdType.MESH
OWN, XSIDE, YSIDE, DIAG = range(4)
ACT, GRAD = range(2)

CHUNK_TIME = 1.4
HOP_TIME = 1.7
POLL_TIME = 0.5
LOAD_TIME = 3.0
UNIT_TIME = 1.0


def route_blocks(line, layers):
    reach = (2 + line) // 3
    even = line % 2 == 0
    free, events, log = {}, [], [[] for _ in range(line)]

    def flipped(at):
        return even and 2 * at > line - 1

    def send(time, at, route, chunk):
        start = max(free.get((at, route), 0.0), time)
        free[at, route] = start + CHUNK_TIME
        there = at + {"x": 0, "y": 0, "up": 1, "down": -1}[route]
        column, plane, which, layer = chunk
        seen = line - 1 - plane if flipped(there) else plane
        role = line - 1 - there if flipped(there) else there
        key = (round(start + CHUNK_TIME + HOP_TIME, 3), role, seen, column, layer, which, there)
        heapq.heappush(events, (key, chunk))

    def passes(at, chunk):
        column, plane, which, layer = chunk
        along = []
        if plane <= at < line - 1:
            along.append(("up", at + 1))
        if plane >= at > 0:
            along.append(("down", at - 1))
        if flipped(at):
            along.reverse()
        distance = abs(plane - at)
        far = distance > reach
        out = []
        if column == OWN:
            out += [(route, chunk) for route, _ in along]
            if plane != at:
                out.append(("y", (YSIDE, plane, which, layer)))
                late = far and layer == layers - 1
                if which == GRAD or not late:
                    out.append(("x", (XSIDE, plane, which, layer)))
                if which == GRAD and late:
                    out.append(("x", (XSIDE, plane, ACT, layer)))
        if column == DIAG:
            out += [(route, chunk) for route, to in along if abs(plane - to) <= reach]
        if far or distance == 0:
            if column == YSIDE and which == ACT:
                out.append(("x", (DIAG, plane, which, layer)))
            if column == XSIDE and which == GRAD:
                out.append(("y", (DIAG, plane, which, layer)))
        return out

    first = []
    for at in range(line):
        mine = []
        for i in range(2 * layers):
            mine += passes(at, (OWN, at, i % 2, i // 2))
            mine.append(("x", (XSIDE, at, 1 - i // layers, i % layers)))
            mine.append(("y", (YSIDE, at, i // layers, i % layers)))
        for route, chunk in mine:
            send(0.0, at, route, chunk)
        first.append(mine)
    while events:
        (time, *_, at), chunk = heapq.heappop(events)
        out = passes(at, chunk)
        for route, sent in out:
            send(time + POLL_TIME, at, route, sent)
        log[at].append((time, chunk, out))
    return first, log


def plan_steps(at, line, layers, log):
    ready = {(OWN, at, layer): 0.0 for layer in range(layers)}
    for time, (column, plane, _, layer), _ in log:
        ready[column, plane, layer] = max(time, ready.get((column, plane, layer), 0.0))
    blocks = sorted(
        {key[:2] for key in ready}, key=lambda b: [ready[(*b, l)] for l in range(layers)][::-1]
    )
    units = []
    for one, two in zip(blocks[::2], blocks[1::2]):
        for layer in range(layers):
            units.append((max(ready[(*one, layer)], ready[(*two, layer)]), one, two, layer))
    units.sort(key=lambda unit: unit[0])
    steps, now, i = [], LOAD_TIME, 0
    for k, (time, one, two, layer) in enumerate(units):
        now = max(now, time)
        moves = []
        while i < len(log) and (log[i][0] <= now or k == len(units) - 1):
            moves.append(log[i][1:])
            i += 1
        steps.append((moves, one, two, layer))
        now += UNIT_TIME
    return steps


def branch(value, low, high, leaf):
    if high - low == 1:
        leaf(low)
        return
    middle = (low + high) // 2
    pl.when(value < middle)(lambda: branch(value, low, middle, leaf))
    pl.when(value >= middle)(lambda: branch(value, middle, high, leaf))


def pick(index, values):
    result = jnp.int32(values[-1])
    for i, value in enumerate(values[:-1]):
        result = jnp.where(index == i, jnp.int32(value), result)
    return result


def kernel(
    layers,
    line,
    train_a,
    train_g,
    test_a,
    test_g,
    ids_ref,
    out_ref,
    ta,
    tg,
    buf,
    acc,
    xbuf,
    train_sem,
    own_sem,
    recv_sem,
    send_sem,
    xs_sem,
    xr_sem,
):
    me = lax.axis_index("tok")
    core = lax.axis_index("layer")
    z = me // 4
    y = (me // 2) % 2
    x = me % 2
    columns = (
        y * 2 + x,
        y * 2 + (1 - x),
        (1 - y) * 2 + x,
        (1 - y) * 2 + (1 - x),
    )
    layer_count, train_rows, _ = ta.shape
    _, rows, width = buf.shape
    q_block = Q // layers
    has_up = z < line - 1
    has_down = z > 0

    roles = line // 2 if line % 2 == 0 else line
    flip = (z >= roles).astype(jnp.int32)
    role = jnp.where(flip == 1, line - 1 - z, z)
    sign = 1 - 2 * flip
    partner = {
        "x": z * 4 + columns[XSIDE],
        "y": z * 4 + columns[YSIDE],
        "up": me + 4 * sign,
        "down": me - 4 * sign,
    }
    routes = tuple(partner)
    across = {
        "x": (XSIDE, OWN, DIAG, YSIDE),
        "y": (YSIDE, DIAG, OWN, XSIDE),
        "up": (OWN, XSIDE, YSIDE, DIAG),
        "down": (OWN, XSIDE, YSIDE, DIAG),
    }

    def place(column, plane):
        return jnp.where(flip == 1, line - 1 - plane, plane) * 4 + columns[column]

    def slot(column, plane, which, layer):
        return (place(column, plane) * layer_count + layer) * 2 + which

    for which, (src, dst) in enumerate(((train_a, ta), (train_g, tg))):
        pltpu.make_async_copy(src, dst, train_sem.at[which]).start()

    def own_copy(which, layer):
        src = (test_a, test_g)[which]
        return pltpu.make_async_copy(
            src.at[layer],
            buf.at[(me * layer_count + layer) * 2 + which],
            own_sem.at[which, layer],
        )

    for which in range(2):
        for layer in range(layer_count):
            own_copy(which, layer).start()

    barrier = pltpu.get_barrier_semaphore()

    def greet(where):
        pl.semaphore_signal(barrier, inc=1, device_id=where, device_id_type=MESH)

    greet({"tok": partner["x"]})
    greet({"tok": partner["y"]})
    pl.when(has_up)(lambda: greet({"tok": me + 4}))
    pl.when(has_down)(lambda: greet({"tok": me - 4}))
    for step in range(1, layers):
        greet({"layer": lax.rem(core + step, layers)})
    ends = jnp.where(has_up, 1, 0) + jnp.where(has_down, 1, 0)
    pl.semaphore_wait(barrier, layers + 1 + ends)

    def copy(route, chunk, src=None):
        column, plane, which, layer = chunk
        here = slot(across[route][column], plane, which, layer)
        return pltpu.make_async_remote_copy(
            src_ref=buf.at[here] if src is None else src,
            dst_ref=buf.at[here],
            send_sem=send_sem.at[routes.index(route)],
            recv_sem=recv_sem.at[here],
            device_id={"tok": partner[route]},
            device_id_type=MESH,
        )

    def arrived(chunk):
        here = slot(*chunk)
        pltpu.make_async_remote_copy(
            src_ref=buf.at[here],
            dst_ref=buf.at[here],
            send_sem=send_sem.at[0],
            recv_sem=recv_sem.at[here],
            device_id={"tok": partner["x"]},
            device_id_type=MESH,
        ).wait_recv()

    first, log = route_blocks(line, layer_count)
    steps = [plan_steps(at, line, layer_count, log[at]) for at in range(roles)]
    count = len(steps[0])

    def send_own(at):
        for route, chunk in first[at]:
            copy(route, chunk, (test_a, test_g)[chunk[2]].at[chunk[3]]).start()

    branch(role, 0, roles, send_own)

    acc[...] = jnp.zeros_like(acc)
    _, tiles, _, tile = xbuf.shape
    labels = lax.broadcasted_iota(jnp.int32, (Q, rows), 0)
    nt = (((1,), (1,)), ((), ()))

    def exchange(step, j):
        to = lax.rem(core + step, layers)
        theirs = pl.ds(pl.multiple_of(to * q_block, q_block), q_block)
        return pltpu.make_async_remote_copy(
            src_ref=acc.at[theirs, pl.ds(pl.multiple_of(j * tile, tile), tile)],
            dst_ref=xbuf.at[step - 1, j],
            send_sem=xs_sem.at[step - 1, j],
            recv_sem=xr_sem.at[step - 1, j],
            device_id={"layer": to},
            device_id_type=MESH,
        )

    for which in range(2):
        for layer in range(layer_count):
            own_copy(which, layer).wait()
    for which, (src, dst) in enumerate(((train_a, ta), (train_g, tg))):
        pltpu.make_async_copy(src, dst, train_sem.at[which]).wait()

    def relay(k, at):
        for chunk, out in steps[at][k][0]:
            arrived(chunk)
            for route, sent in out:
                copy(route, sent).start()

    base = line * 4
    packed = [
        (
            ((one[1] * 4 + one[0]) * base + two[1] * 4 + two[0]) * layer_count + layer
        )
        for at in range(roles)
        for _, one, two, layer in steps[at]
    ]

    def position(code):
        plane, column = code // 4, code % 4
        plane = jnp.where(flip == 1, line - 1 - plane, plane)
        return plane * 4 + pick(column, columns)

    def step(k, carry):
        branch(k, 0, count, lambda k0: branch(role, 0, roles, functools.partial(relay, k0)))
        code = pick(role * count + k, packed)
        layer = code % layer_count
        one = position(code // layer_count // base)
        two = position((code // layer_count) % base)
        select = jnp.concatenate(
            [
                jnp.where(ids_ref[b] == labels, 1.0, 0.0).astype(jnp.bfloat16)
                for b in (one, two)
            ],
            axis=1,
        )

        def held(which):
            return jnp.concatenate(
                [buf[(b * layer_count + layer) * 2 + which] for b in (one, two)], axis=0
            )

        def one_tile(j, carry):
            at = pl.ds(pl.multiple_of(j * tile, tile), tile)
            a_gram = lax.dot_general(
                held(ACT), ta[layer, at, :], nt, preferred_element_type=jnp.float32
            )
            g_gram = lax.dot_general(
                held(GRAD), tg[layer, at, :], nt, preferred_element_type=jnp.float32
            )
            product = (a_gram * g_gram).astype(jnp.bfloat16)
            acc[:, at] += jnp.dot(select, product, preferred_element_type=jnp.float32)

            @pl.when(k == count - 1)
            def _():
                for step in range(1, layers):
                    exchange(step, j).start()

            return carry

        lax.fori_loop(0, tiles, one_tile, 0)
        return carry

    lax.fori_loop(0, count, step, 0)

    def drain(at):
        sent = list(first[at])
        for moves, *_ in steps[at]:
            for _, out in moves:
                sent += out
        for i, route in enumerate(routes):
            total = sum(r == route for r, _ in sent)
            if total > 0:
                all_of_them = buf.at[pl.ds(0, total)]
                pltpu.make_async_remote_copy(
                    src_ref=all_of_them,
                    dst_ref=all_of_them,
                    send_sem=send_sem.at[i],
                    recv_sem=recv_sem.at[0],
                    device_id={"tok": partner["x"]},
                    device_id_type=MESH,
                ).wait_send()

    branch(role, 0, roles, drain)

    mine = pl.ds(pl.multiple_of(core * q_block, q_block), q_block)
    for j in range(tiles):
        at = pl.ds(j * tile, tile)
        for step in range(1, layers):
            exchange(step, j).wait_recv()
        result = acc[mine, at]
        for step in range(1, layers):
            result = result + xbuf[step - 1, j]
        out_ref[:, at] = result
    for j in range(tiles):
        for step in range(1, layers):
            exchange(step, j).wait_send()


def on_device(layers, toks, train_act, train_grad, test_act, test_grad, segment_ids):
    layer_count, train_rows, width = train_act.shape
    rows = test_act.shape[1]
    line = toks // 4
    tile = math.gcd(train_rows, 1024)
    tiles = train_rows // tile
    q_block = Q // layers
    ids = segment_ids.reshape(toks, 1, rows)
    dma = pltpu.SemaphoreType.DMA
    anywhere = pl.BlockSpec(memory_space=pl.ANY)
    return pl.pallas_call(
        functools.partial(kernel, layers, line),
        out_shape=jax.ShapeDtypeStruct((q_block, train_rows), jnp.float32),
        in_specs=[anywhere] * 4 + [pl.BlockSpec(memory_space=pltpu.VMEM)],
        out_specs=pl.BlockSpec(memory_space=pltpu.VMEM),
        scratch_shapes=[
            pltpu.VMEM((layer_count, train_rows, width), jnp.bfloat16),
            pltpu.VMEM((layer_count, train_rows, width), jnp.bfloat16),
            pltpu.VMEM((toks * layer_count * 2, rows, width), jnp.bfloat16),
            pltpu.VMEM((Q, train_rows), jnp.float32),
            pltpu.VMEM((layers - 1, tiles, q_block, tile), jnp.float32),
            dma((2,)),
            dma((2, layer_count)),
            dma((toks * layer_count * 2,)),
            dma((4,)),
            dma((layers - 1, tiles)),
            dma((layers - 1, tiles)),
        ],
        compiler_params=pltpu.CompilerParams(
            collective_id=0, has_side_effects=True, vmem_limit_bytes=63 * 1024 * 1024
        ),
    )(train_act, train_grad, test_act, test_grad, ids)


def solution(mesh):
    placed = (
        P("layer", "tok", None),
        P("layer", "tok", None),
        P("layer", "tok", None),
        P("layer", "tok", None),
        P(),
    )
    body = functools.partial(on_device, mesh.shape["layer"], mesh.shape["tok"])
    return jax.shard_map(
        body, mesh=mesh, in_specs=placed, out_specs=P("layer", "tok"), check_vma=False
    )
```

time: 46.7 us -> 42.9 us (0.919)
  Pallas kernels: 44.7 us -> 40.8 us
    pallas_call x1, Pallas kernels: 44.7 us -> 40.8 us  [on_device(): pl.pallas_call(functools.partial(kernel, layers, line), out_shape=jax.Sha...]
where the time goes in v1:
time: 42.9 us; the launch traced here: 42.7 us
  Pallas kernels  40.8 us (95%)
  local copies, waits for them, and re-layouts  1.87 us (4%)
    pallas_call x1, Pallas kernels, on_device(): pl.pallas_call(functools.partial(kernel, layers, line), out_shape=jax.Sha...  40.8 us
    unnamed x1, local copies, waits for them, and re-layouts  1.87 us

profile of v1, /device:TPU:0, one launch (start us, length us, event | category | flops | bytes accessed | tf_op | source)
XLA Modules:
  0.0 42.7 jit_solution(12596309343122467962)
XLA Ops:
  0.0 40.8 %shard_map.55 = f32[64,2048]{1,0:T(8,128)} custom-call(bf16[2,2048,256]{2,1,0:T(8,128)(2,1)} %train_a.1, bf16[2,2048,256]{2,1,0:T(8,128)(2,1)} %train_g.1, bf16[2,128,256]{2,1,0:T(8,128)(2,1)} %test_a.1, bf16[2,128,256]{2,1,0:T(8,128)(2,1)} %test_g.1, s32[16,1,128]{2,1,0:T(1,128)} %bitcast.1), custom_call_target="tpu_custom_call" | custom-call | tf_op jit(solution)/shard_map/pallas_call | solution.py:384
  40.8 1.9 %copy.7 = f32[64,2048]{1,0:T(8,128)} copy(f32[64,2048]{1,0:T(8,128)} %shard_map.55) | data formatting | bytes 1048576

commit v2 on v1

--- a/solution.py
+++ b/solution.py
@@ -13,6 +13,8 @@
 MESH = pl.DeviceIdType.MESH
 OWN, XSIDE, YSIDE, DIAG = range(4)
 ACT, GRAD = range(2)
+
+LIMIT = 60 * 1024 * 1024
 
 CHUNK_TIME = 1.4
 HOP_TIME = 1.7
@@ -104,8 +106,9 @@
     for k, (time, one, two, layer) in enumerate(units):
         now = max(now, time)
         moves = []
-        while i < len(log) and (log[i][0] <= now or k == len(units) - 1):
+        while i < len(log) and (log[i][0] <= now + 0.8 or k == len(units) - 1):
             moves.append(log[i][1:])
+            now = max(now, log[i][0])
             i += 1
         steps.append((moves, one, two, layer))
         now += UNIT_TIME
@@ -135,13 +138,16 @@
     train_g,
     test_a,
     test_g,
+    ids_hbm,
+    out_ref,
     ids_ref,
-    out_ref,
+    prod,
     ta,
     tg,
     buf,
     acc,
     xbuf,
+    xout,
     train_sem,
     own_sem,
     recv_sem,
@@ -190,8 +196,6 @@
     def slot(column, plane, which, layer):
         return (place(column, plane) * layer_count + layer) * 2 + which
 
-    for which, (src, dst) in enumerate(((train_a, ta), (train_g, tg))):
-        pltpu.make_async_copy(src, dst, train_sem.at[which]).start()
 
     def own_copy(which, layer):
         src = (test_a, test_g)[which]
@@ -204,6 +208,8 @@
     for which in range(2):
         for layer in range(layer_count):
             own_copy(which, layer).start()
+    ids_copy = pltpu.make_async_copy(ids_hbm, ids_ref, train_sem.at[2])
+    ids_copy.start()
 
     barrier = pltpu.get_barrier_semaphore()
 
@@ -252,6 +258,9 @@
 
     branch(role, 0, roles, send_own)
 
+    for which, (src, dst) in enumerate(((train_a, ta), (train_g, tg))):
+        pltpu.make_async_copy(src, dst, train_sem.at[which]).start()
+
     acc[...] = jnp.zeros_like(acc)
     _, tiles, _, tile = xbuf.shape
     labels = lax.broadcasted_iota(jnp.int32, (Q, rows), 0)
@@ -259,9 +268,8 @@
 
     def exchange(step, j):
         to = lax.rem(core + step, layers)
-        theirs = pl.ds(pl.multiple_of(to * q_block, q_block), q_block)
         return pltpu.make_async_remote_copy(
-            src_ref=acc.at[theirs, pl.ds(pl.multiple_of(j * tile, tile), tile)],
+            src_ref=xout.at[step - 1, j],
             dst_ref=xbuf.at[step - 1, j],
             send_sem=xs_sem.at[step - 1, j],
             recv_sem=xr_sem.at[step - 1, j],
@@ -269,6 +277,7 @@
             device_id_type=MESH,
         )
 
+    ids_copy.wait()
     for which in range(2):
         for layer in range(layer_count):
             own_copy(which, layer).wait()
@@ -314,25 +323,24 @@
                 [buf[(b * layer_count + layer) * 2 + which] for b in (one, two)], axis=0
             )
 
-        def one_tile(j, carry):
-            at = pl.ds(pl.multiple_of(j * tile, tile), tile)
-            a_gram = lax.dot_general(
-                held(ACT), ta[layer, at, :], nt, preferred_element_type=jnp.float32
-            )
-            g_gram = lax.dot_general(
-                held(GRAD), tg[layer, at, :], nt, preferred_element_type=jnp.float32
-            )
-            product = (a_gram * g_gram).astype(jnp.bfloat16)
-            acc[:, at] += jnp.dot(select, product, preferred_element_type=jnp.float32)
-
-            @pl.when(k == count - 1)
-            def _():
+        a_held, g_held = held(ACT), held(GRAD)
+        one_q = jnp.where(ids_ref[one] == labels, 1.0, 0.0).astype(jnp.bfloat16)
+
+        a_gram = lax.dot_general(a_held, ta[layer], nt, preferred_element_type=jnp.float32)
+        g_gram = lax.dot_general(g_held, tg[layer], nt, preferred_element_type=jnp.float32)
+        prod[...] = (a_gram * g_gram).astype(jnp.bfloat16)
+
+        acc[...] += jnp.dot(select, prod[...], preferred_element_type=jnp.float32)
+
+        @pl.when(k == count - 1)
+        def _():
+            for j in range(tiles):
                 for step in range(1, layers):
+                    theirs = lax.rem(core + step, layers) * q_block
+                    xout[step - 1, j] = acc[
+                        pl.ds(pl.multiple_of(theirs, q_block), q_block), pl.ds(j * tile, tile)
+                    ].astype(jnp.bfloat16)
                     exchange(step, j).start()
-
-            return carry
-
-        lax.fori_loop(0, tiles, one_tile, 0)
         return carry
 
     lax.fori_loop(0, count, step, 0)
@@ -364,7 +372,7 @@
             exchange(step, j).wait_recv()
         result = acc[mine, at]
         for step in range(1, layers):
-            result = result + xbuf[step - 1, j]
+            result = result + xbuf[step - 1, j].astype(jnp.float32)
         out_ref[:, at] = result
     for j in range(tiles):
         for step in range(1, layers):
@@ -380,19 +388,22 @@
     q_block = Q // layers
     ids = segment_ids.reshape(toks, 1, rows)
     dma = pltpu.SemaphoreType.DMA
-    anywhere = pl.BlockSpec(memory_space=pl.ANY)
+    in_hbm = pl.BlockSpec(memory_space=pltpu.HBM)
     return pl.pallas_call(
         functools.partial(kernel, layers, line),
-        out_shape=jax.ShapeDtypeStruct((q_block, train_rows), jnp.float32),
-        in_specs=[anywhere] * 4 + [pl.BlockSpec(memory_space=pltpu.VMEM)],
+        out_shape=pltpu.VMEM((q_block, train_rows), jnp.float32),
+        in_specs=[in_hbm] * 5,
         out_specs=pl.BlockSpec(memory_space=pltpu.VMEM),
         scratch_shapes=[
+            pltpu.VMEM((toks, 1, rows), jnp.int32),
+            pltpu.VMEM((2 * rows, train_rows), jnp.bfloat16),
             pltpu.VMEM((layer_count, train_rows, width), jnp.bfloat16),
             pltpu.VMEM((layer_count, train_rows, width), jnp.bfloat16),
             pltpu.VMEM((toks * layer_count * 2, rows, width), jnp.bfloat16),
             pltpu.VMEM((Q, train_rows), jnp.float32),
-            pltpu.VMEM((layers - 1, tiles, q_block, tile), jnp.float32),
-            dma((2,)),
+            pltpu.VMEM((layers - 1, tiles, q_block, tile), jnp.bfloat16),
+            pltpu.VMEM((layers - 1, tiles, q_block, tile), jnp.bfloat16),
+            dma((3,)),
             dma((2, layer_count)),
             dma((toks * layer_count * 2,)),
             dma((4,)),
@@ -400,7 +411,7 @@
             dma((layers - 1, tiles)),
         ],
         compiler_params=pltpu.CompilerParams(
-            collective_id=0, has_side_effects=True, vmem_limit_bytes=63 * 1024 * 1024
+            collective_id=0, has_side_effects=True, vmem_limit_bytes=LIMIT
         ),
     )(train_act, train_grad, test_act, test_grad, ids)
 

time: 42.9 us -> 38 us (0.89)
  Pallas kernels: 40.8 us -> 37 us
  local copies, waits for them, and re-layouts: 1.87 us -> 0.8 us
    pallas_call x1, Pallas kernels: 40.8 us -> 37 us  [on_device(): pl.pallas_call(functools.partial(kernel, layers, line), out_shape=pltpu.V...]
    unnamed x1, local copies, waits for them, and re-layouts: 1.87 us -> 0.8 us
where the time goes in v2:
time: 38 us; the launch traced here: 37.8 us
  Pallas kernels  37 us (97%)
  local copies, waits for them, and re-layouts  0.8 us (2%)
    pallas_call x1, Pallas kernels, on_device(): pl.pallas_call(functools.partial(kernel, layers, line), out_shape=pltpu.V...  37 us
    unnamed x1, local copies, waits for them, and re-layouts  0.8 us

profile of v2, /device:TPU:0, one launch (start us, length us, event | category | flops | bytes accessed | tf_op | source)
XLA Modules:
  0.0 37.8 jit_solution(8663268629979659896)
XLA Ops:
  0.0 37.0 %shard_map.55 = f32[64,2048]{1,0:T(8,128)S(1)} custom-call(bf16[2,2048,256]{2,1,0:T(8,128)(2,1)} %train_a.1, bf16[2,2048,256]{2,1,0:T(8,128)(2,1)} %train_g.1, bf16[2,128,256]{2,1,0:T(8,128)(2,1)} %test_a.1, bf16[2,128,256]{2,1,0:T(8,128)(2,1)} %test_g.1, s32[16,1,128]{2,1,0:T(1,128)} %bitcast.1), custom_call_target="tpu_custom_call" | custom-call | tf_op jit(solution)/shard_map/pallas_call | solution.py:392
  37.0 0.8 %copy.7 = f32[64,2048]{1,0:T(8,128)} copy(f32[64,2048]{1,0:T(8,128)S(1)} %shard_map.55) | data formatting | bytes 1048576

commit v3 on v2

--- a/solution.py
+++ b/solution.py
@@ -19,6 +19,8 @@
 CHUNK_TIME = 1.4
 HOP_TIME = 1.7
 POLL_TIME = 0.5
+GROUP_TIME = 0.3
+AHEAD_TIME = 0.8
 LOAD_TIME = 3.0
 UNIT_TIME = 1.0
 
@@ -90,10 +92,21 @@
     return first, log
 
 
-def plan_steps(at, line, layers, log):
+def gather_groups(log):
+    groups, opened = [], 0.0
+    for time, chunk, out in log:
+        if not groups or time > opened + GROUP_TIME:
+            groups.append([])
+            opened = time
+        groups[-1].append((time, chunk, out))
+    return groups
+
+
+def plan_steps(at, layers, groups):
     ready = {(OWN, at, layer): 0.0 for layer in range(layers)}
-    for time, (column, plane, _, layer), _ in log:
-        ready[column, plane, layer] = max(time, ready.get((column, plane, layer), 0.0))
+    for group in groups:
+        for _, (column, plane, _, layer), _ in group:
+            ready[column, plane, layer] = group[-1][0]
     blocks = sorted(
         {key[:2] for key in ready}, key=lambda b: [ready[(*b, l)] for l in range(layers)][::-1]
     )
@@ -106,9 +119,11 @@
     for k, (time, one, two, layer) in enumerate(units):
         now = max(now, time)
         moves = []
-        while i < len(log) and (log[i][0] <= now + 0.8 or k == len(units) - 1):
-            moves.append(log[i][1:])
-            now = max(now, log[i][0])
+        while i < len(groups) and (
+            groups[i][-1][0] <= now + AHEAD_TIME or k == len(units) - 1
+        ):
+            now = max(now, groups[i][-1][0])
+            moves.append(i)
             i += 1
         steps.append((moves, one, two, layer))
         now += UNIT_TIME
@@ -134,6 +149,8 @@
 def kernel(
     layers,
     line,
+    first,
+    groups,
     train_a,
     train_g,
     test_a,
@@ -142,8 +159,7 @@
     out_ref,
     ids_ref,
     prod,
-    ta,
-    tg,
+    train,
     buf,
     acc,
     xbuf,
@@ -166,7 +182,7 @@
         (1 - y) * 2 + x,
         (1 - y) * 2 + (1 - x),
     )
-    layer_count, train_rows, _ = ta.shape
+    _, layer_count, train_rows, _ = train.shape
     _, rows, width = buf.shape
     q_block = Q // layers
     has_up = z < line - 1
@@ -183,6 +199,18 @@
         "down": me - 4 * sign,
     }
     routes = tuple(partner)
+    group_of = [
+        {chunk: i for i, group in enumerate(groups[at]) for _, chunk, _ in group}
+        for at in range(roles)
+    ]
+
+    def group_there(at, route, chunk):
+        column, plane, which, layer = chunk
+        there = at + {"x": 0, "y": 0, "up": 1, "down": -1}[route]
+        if there >= roles:
+            there, plane = line - 1 - there, line - 1 - plane
+        return group_of[there][column, plane, which, layer]
+
     across = {
         "x": (XSIDE, OWN, DIAG, YSIDE),
         "y": (YSIDE, DIAG, OWN, XSIDE),
@@ -202,13 +230,13 @@
         return pltpu.make_async_copy(
             src.at[layer],
             buf.at[(me * layer_count + layer) * 2 + which],
-            own_sem.at[which, layer],
+            own_sem.at[0],
         )
 
     for which in range(2):
         for layer in range(layer_count):
             own_copy(which, layer).start()
-    ids_copy = pltpu.make_async_copy(ids_hbm, ids_ref, train_sem.at[2])
+    ids_copy = pltpu.make_async_copy(ids_hbm, ids_ref, train_sem.at[1])
     ids_copy.start()
 
     barrier = pltpu.get_barrier_semaphore()
@@ -225,41 +253,39 @@
     ends = jnp.where(has_up, 1, 0) + jnp.where(has_down, 1, 0)
     pl.semaphore_wait(barrier, layers + 1 + ends)
 
-    def copy(route, chunk, src=None):
+    def copy(at, route, chunk, src=None):
         column, plane, which, layer = chunk
         here = slot(across[route][column], plane, which, layer)
         return pltpu.make_async_remote_copy(
             src_ref=buf.at[here] if src is None else src,
             dst_ref=buf.at[here],
             send_sem=send_sem.at[routes.index(route)],
-            recv_sem=recv_sem.at[here],
+            recv_sem=recv_sem.at[group_there(at, route, chunk)],
             device_id={"tok": partner[route]},
             device_id_type=MESH,
         )
 
-    def arrived(chunk):
-        here = slot(*chunk)
+    def arrived(index, size):
         pltpu.make_async_remote_copy(
-            src_ref=buf.at[here],
-            dst_ref=buf.at[here],
+            src_ref=buf.at[pl.ds(0, size)],
+            dst_ref=buf.at[pl.ds(0, size)],
             send_sem=send_sem.at[0],
-            recv_sem=recv_sem.at[here],
+            recv_sem=recv_sem.at[index],
             device_id={"tok": partner["x"]},
             device_id_type=MESH,
         ).wait_recv()
 
-    first, log = route_blocks(line, layer_count)
-    steps = [plan_steps(at, line, layer_count, log[at]) for at in range(roles)]
+    steps = [plan_steps(at, layer_count, groups[at]) for at in range(roles)]
     count = len(steps[0])
 
     def send_own(at):
         for route, chunk in first[at]:
-            copy(route, chunk, (test_a, test_g)[chunk[2]].at[chunk[3]]).start()
+            copy(at, route, chunk, (test_a, test_g)[chunk[2]].at[chunk[3]]).start()
 
     branch(role, 0, roles, send_own)
 
-    for which, (src, dst) in enumerate(((train_a, ta), (train_g, tg))):
-        pltpu.make_async_copy(src, dst, train_sem.at[which]).start()
+    for which, src in enumerate((train_a, train_g)):
+        pltpu.make_async_copy(src, train.at[which], train_sem.at[0]).start()
 
     acc[...] = jnp.zeros_like(acc)
     _, tiles, _, tile = xbuf.shape
@@ -278,17 +304,17 @@
         )
 
     ids_copy.wait()
-    for which in range(2):
-        for layer in range(layer_count):
-            own_copy(which, layer).wait()
-    for which, (src, dst) in enumerate(((train_a, ta), (train_g, tg))):
-        pltpu.make_async_copy(src, dst, train_sem.at[which]).wait()
+    own_all = buf.at[pl.ds(me * layer_count * 2, layer_count * 2)]
+    pltpu.make_async_copy(own_all, own_all, own_sem.at[0]).wait()
+    pltpu.make_async_copy(train, train, train_sem.at[0]).wait()
 
     def relay(k, at):
-        for chunk, out in steps[at][k][0]:
-            arrived(chunk)
-            for route, sent in out:
-                copy(route, sent).start()
+        for index in steps[at][k][0]:
+            group = groups[at][index]
+            arrived(index, len(group))
+            for _, _, out in group:
+                for route, sent in out:
+                    copy(at, route, sent).start()
 
     base = line * 4
     packed = [
@@ -326,8 +352,8 @@
         a_held, g_held = held(ACT), held(GRAD)
         one_q = jnp.where(ids_ref[one] == labels, 1.0, 0.0).astype(jnp.bfloat16)
 
-        a_gram = lax.dot_general(a_held, ta[layer], nt, preferred_element_type=jnp.float32)
-        g_gram = lax.dot_general(g_held, tg[layer], nt, preferred_element_type=jnp.float32)
+        a_gram = lax.dot_general(a_held, train[ACT, layer], nt, preferred_element_type=jnp.float32)
+        g_gram = lax.dot_general(g_held, train[GRAD, layer], nt, preferred_element_type=jnp.float32)
         prod[...] = (a_gram * g_gram).astype(jnp.bfloat16)
 
         acc[...] += jnp.dot(select, prod[...], preferred_element_type=jnp.float32)
@@ -347,8 +373,8 @@
 
     def drain(at):
         sent = list(first[at])
-        for moves, *_ in steps[at]:
-            for _, out in moves:
+        for group in groups[at]:
+            for _, _, out in group:
                 sent += out
         for i, route in enumerate(routes):
             total = sum(r == route for r, _ in sent)
@@ -383,29 +409,30 @@
     layer_count, train_rows, width = train_act.shape
     rows = test_act.shape[1]
     line = toks // 4
-    tile = math.gcd(train_rows, 1024)
+    first, log = route_blocks(line, layer_count)
+    groups = [gather_groups(received) for received in log]
+    tile = math.gcd(train_rows, 2048)
     tiles = train_rows // tile
     q_block = Q // layers
     ids = segment_ids.reshape(toks, 1, rows)
     dma = pltpu.SemaphoreType.DMA
     in_hbm = pl.BlockSpec(memory_space=pltpu.HBM)
     return pl.pallas_call(
-        functools.partial(kernel, layers, line),
+        functools.partial(kernel, layers, line, first, groups),
         out_shape=pltpu.VMEM((q_block, train_rows), jnp.float32),
         in_specs=[in_hbm] * 5,
         out_specs=pl.BlockSpec(memory_space=pltpu.VMEM),
         scratch_shapes=[
             pltpu.VMEM((toks, 1, rows), jnp.int32),
             pltpu.VMEM((2 * rows, train_rows), jnp.bfloat16),
-            pltpu.VMEM((layer_count, train_rows, width), jnp.bfloat16),
-            pltpu.VMEM((layer_count, train_rows, width), jnp.bfloat16),
+            pltpu.VMEM((2, layer_count, train_rows, width), jnp.bfloat16),
             pltpu.VMEM((toks * layer_count * 2, rows, width), jnp.bfloat16),
             pltpu.VMEM((Q, train_rows), jnp.float32),
             pltpu.VMEM((layers - 1, tiles, q_block, tile), jnp.bfloat16),
             pltpu.VMEM((layers - 1, tiles, q_block, tile), jnp.bfloat16),
-            dma((3,)),
-            dma((2, layer_count)),
-            dma((toks * layer_count * 2,)),
+            dma((2,)),
+            dma((1,)),
+            dma((max(len(g) for g in groups),)),
             dma((4,)),
             dma((layers - 1, tiles)),
             dma((layers - 1, tiles)),

time: 38 us -> 37.5 us (0.987)
  Pallas kernels: 37 us -> 36.6 us
    pallas_call x1, Pallas kernels: 37 us -> 36.6 us  [on_device(): pl.pallas_call(functools.partial(kernel, layers, line, first, groups), ou...]
where the time goes in v3:
time: 37.5 us; the launch traced here: 37.4 us
  Pallas kernels  36.6 us (98%)
  local copies, waits for them, and re-layouts  0.8 us (2%)
    pallas_call x1, Pallas kernels, on_device(): pl.pallas_call(functools.partial(kernel, layers, line, first, groups), ou...  36.6 us
    unnamed x1, local copies, waits for them, and re-layouts  0.8 us

profile of v3, /device:TPU:0, one launch (start us, length us, event | category | flops | bytes accessed | tf_op | source)
XLA Modules:
  0.0 37.4 jit_solution(2722851028544793417)
XLA Ops:
  0.0 36.6 %shard_map.55 = f32[64,2048]{1,0:T(8,128)S(1)} custom-call(bf16[2,2048,256]{2,1,0:T(8,128)(2,1)} %train_a.1, bf16[2,2048,256]{2,1,0:T(8,128)(2,1)} %train_g.1, bf16[2,128,256]{2,1,0:T(8,128)(2,1)} %test_a.1, bf16[2,128,256]{2,1,0:T(8,128)(2,1)} %test_g.1, s32[16,1,128]{2,1,0:T(1,128)} %bitcast.1), custom_call_target="tpu_custom_call" | custom-call | tf_op jit(solution)/shard_map/pallas_call | solution.py:420
  36.6 0.8 %copy.7 = f32[64,2048]{1,0:T(8,128)} copy(f32[64,2048]{1,0:T(8,128)S(1)} %shard_map.55) | data formatting | bytes 1048576

commit v4 on v3

--- a/solution.py
+++ b/solution.py
@@ -168,6 +168,7 @@
     own_sem,
     recv_sem,
     send_sem,
+    ready_sem,
     xs_sem,
     xr_sem,
 ):
@@ -239,19 +240,22 @@
     ids_copy = pltpu.make_async_copy(ids_hbm, ids_ref, train_sem.at[1])
     ids_copy.start()
 
+    lower = {"x": x == 1, "y": y == 1, "up": flip == 1, "down": flip == 0}
+    axis = {"x": 0, "y": 1, "up": 2, "down": 2}
     barrier = pltpu.get_barrier_semaphore()
 
-    def greet(where):
-        pl.semaphore_signal(barrier, inc=1, device_id=where, device_id_type=MESH)
-
-    greet({"tok": partner["x"]})
-    greet({"tok": partner["y"]})
+    def greet(where, semaphore=barrier):
+        pl.semaphore_signal(semaphore, inc=1, device_id=where, device_id_type=MESH)
+
+    pl.when(x == 0)(lambda: greet({"tok": partner["x"]}))
+    pl.when(y == 0)(lambda: greet({"tok": partner["y"]}))
     pl.when(has_up)(lambda: greet({"tok": me + 4}))
-    pl.when(has_down)(lambda: greet({"tok": me - 4}))
     for step in range(1, layers):
         greet({"layer": lax.rem(core + step, layers)})
-    ends = jnp.where(has_up, 1, 0) + jnp.where(has_down, 1, 0)
-    pl.semaphore_wait(barrier, layers + 1 + ends)
+    pl.semaphore_wait(barrier, layers - 1 + x + y + has_down.astype(jnp.int32))
+    pl.when(x == 1)(lambda: greet({"tok": partner["x"]}, ready_sem.at[0]))
+    pl.when(y == 1)(lambda: greet({"tok": partner["y"]}, ready_sem.at[1]))
+    pl.when(has_down)(lambda: greet({"tok": me - 4}, ready_sem.at[2]))
 
     def copy(at, route, chunk, src=None):
         column, plane, which, layer = chunk
@@ -279,8 +283,21 @@
     count = len(steps[0])
 
     def send_own(at):
-        for route, chunk in first[at]:
-            copy(at, route, chunk, (test_a, test_g)[chunk[2]].at[chunk[3]]).start()
+        def send(route):
+            for own_route, chunk in first[at]:
+                if own_route == route:
+                    src = (test_a, test_g)[chunk[2]].at[chunk[3]]
+                    copy(at, route, chunk, src).start()
+
+        def answered(route):
+            pl.semaphore_wait(ready_sem.at[axis[route]], 1)
+            send(route)
+
+        used = sorted({route for route, _ in first[at]}, key=routes.index)
+        for route in used:
+            pl.when(lower[route])(functools.partial(send, route))
+        for route in used:
+            pl.when(jnp.logical_not(lower[route]))(functools.partial(answered, route))
 
     branch(role, 0, roles, send_own)
 
@@ -331,7 +348,6 @@
         return plane * 4 + pick(column, columns)
 
     def step(k, carry):
-        branch(k, 0, count, lambda k0: branch(role, 0, roles, functools.partial(relay, k0)))
         code = pick(role * count + k, packed)
         layer = code % layer_count
         one = position(code // layer_count // base)
@@ -344,13 +360,14 @@
             axis=1,
         )
 
+        branch(k, 0, count, lambda k0: branch(role, 0, roles, functools.partial(relay, k0)))
+
         def held(which):
             return jnp.concatenate(
                 [buf[(b * layer_count + layer) * 2 + which] for b in (one, two)], axis=0
             )
 
         a_held, g_held = held(ACT), held(GRAD)
-        one_q = jnp.where(ids_ref[one] == labels, 1.0, 0.0).astype(jnp.bfloat16)
 
         a_gram = lax.dot_general(a_held, train[ACT, layer], nt, preferred_element_type=jnp.float32)
         g_gram = lax.dot_general(g_held, train[GRAD, layer], nt, preferred_element_type=jnp.float32)
@@ -434,6 +451,7 @@
             dma((1,)),
             dma((max(len(g) for g in groups),)),
             dma((4,)),
+            pltpu.SemaphoreType.REGULAR((3,)),
             dma((layers - 1, tiles)),
             dma((layers - 1, tiles)),
         ],

time: 37.5 us -> 36.9 us (0.984)
  Pallas kernels: 36.6 us -> 36 us
    pallas_call x1, Pallas kernels: 36.6 us -> 36 us  [on_device(): pl.pallas_call(functools.partial(kernel, layers, line, first, groups), ou...]
where the time goes in v4:
time: 36.9 us; the launch traced here: 36.8 us
  Pallas kernels  36 us (98%)
  local copies, waits for them, and re-layouts  0.8 us (2%)
    pallas_call x1, Pallas kernels, on_device(): pl.pallas_call(functools.partial(kernel, layers, line, first, groups), ou...  36 us
    unnamed x1, local copies, waits for them, and re-layouts  0.8 us

profile of v4, /device:TPU:0, one launch (start us, length us, event | category | flops | bytes accessed | tf_op | source)
XLA Modules:
  0.0 36.8 jit_solution(8142633975090046241)
XLA Ops:
  0.0 36.0 %shard_map.55 = f32[64,2048]{1,0:T(8,128)S(1)} custom-call(bf16[2,2048,256]{2,1,0:T(8,128)(2,1)} %train_a.1, bf16[2,2048,256]{2,1,0:T(8,128)(2,1)} %train_g.1, bf16[2,128,256]{2,1,0:T(8,128)(2,1)} %test_a.1, bf16[2,128,256]{2,1,0:T(8,128)(2,1)} %test_g.1, s32[16,1,128]{2,1,0:T(1,128)} %bitcast.1), custom_call_target="tpu_custom_call" | custom-call | tf_op jit(solution)/shard_map/pallas_call | solution.py:437
  36.0 0.8 %copy.7 = f32[64,2048]{1,0:T(8,128)} copy(f32[64,2048]{1,0:T(8,128)S(1)} %shard_map.55) | data formatting | bytes 1048576

commit v5 on v4

--- a/solution.py
+++ b/solution.py
@@ -20,7 +20,7 @@
 HOP_TIME = 1.7
 POLL_TIME = 0.5
 GROUP_TIME = 0.3
-AHEAD_TIME = 0.8
+AHEAD_TIME = 0.5
 LOAD_TIME = 3.0
 UNIT_TIME = 1.0
 
@@ -29,6 +29,9 @@
     reach = (2 + line) // 3
     even = line % 2 == 0
     free, events, log = {}, [], [[] for _ in range(line)]
+    expected = {(at, "up"): 2 * layers * at for at in range(line)}
+    expected |= {(at, "down"): 2 * layers * (line - 1 - at) for at in range(line)}
+    held = {key: [] for key in expected}
 
     def flipped(at):
         return even and 2 * at > line - 1
@@ -58,6 +61,10 @@
         if column == OWN:
             out += [(route, chunk) for route, _ in along]
             if plane != at:
+                for route, _ in along:
+                    expected[at, route] -= 1
+                    if expected[at, route] == 0:
+                        out += held[at, route]
                 out.append(("y", (YSIDE, plane, which, layer)))
                 late = far and layer == layers - 1
                 if which == GRAD or not late:
@@ -65,7 +72,10 @@
                 if which == GRAD and late:
                     out.append(("x", (XSIDE, plane, ACT, layer)))
         if column == DIAG:
-            out += [(route, chunk) for route, to in along if abs(plane - to) <= reach]
+            for route, to in along:
+                if abs(plane - to) <= reach:
+                    wait = expected[at, route] > 0
+                    (held[at, route] if wait else out).append((route, chunk))
         if far or distance == 0:
             if column == YSIDE and which == ACT:
                 out.append(("x", (DIAG, plane, which, layer)))
@@ -250,12 +260,15 @@
     pl.when(x == 0)(lambda: greet({"tok": partner["x"]}))
     pl.when(y == 0)(lambda: greet({"tok": partner["y"]}))
     pl.when(has_up)(lambda: greet({"tok": me + 4}))
-    for step in range(1, layers):
-        greet({"layer": lax.rem(core + step, layers)})
-    pl.semaphore_wait(barrier, layers - 1 + x + y + has_down.astype(jnp.int32))
+    for other in range(layers):
+        pl.when(other > core)(functools.partial(greet, {"layer": other}))
+    before = core + x + y + has_down.astype(jnp.int32)
+    pl.when(before > 0)(lambda: pl.semaphore_wait(barrier, before))
     pl.when(x == 1)(lambda: greet({"tok": partner["x"]}, ready_sem.at[0]))
     pl.when(y == 1)(lambda: greet({"tok": partner["y"]}, ready_sem.at[1]))
     pl.when(has_down)(lambda: greet({"tok": me - 4}, ready_sem.at[2]))
+    for other in range(layers):
+        pl.when(other < core)(functools.partial(greet, {"layer": other}, ready_sem.at[3]))
 
     def copy(at, route, chunk, src=None):
         column, plane, which, layer = chunk
@@ -304,6 +317,8 @@
     for which, src in enumerate((train_a, train_g)):
         pltpu.make_async_copy(src, train.at[which], train_sem.at[0]).start()
 
+    after = layers - 1 - core
+    pl.when(after > 0)(lambda: pl.semaphore_wait(ready_sem.at[3], after))
     acc[...] = jnp.zeros_like(acc)
     _, tiles, _, tile = xbuf.shape
     labels = lax.broadcasted_iota(jnp.int32, (Q, rows), 0)
@@ -451,7 +466,7 @@
             dma((1,)),
             dma((max(len(g) for g in groups),)),
             dma((4,)),
-            pltpu.SemaphoreType.REGULAR((3,)),
+            pltpu.SemaphoreType.REGULAR((4,)),
             dma((layers - 1, tiles)),
             dma((layers - 1, tiles)),
         ],

time: 36.9 us -> 36.5 us (0.989)
  Pallas kernels: 36 us -> 35.6 us
    pallas_call x1, Pallas kernels: 36 us -> 35.6 us  [on_device(): pl.pallas_call(functools.partial(kernel, layers, line, first, groups), ou...]
where the time goes in v5:
time: 36.5 us; the launch traced here: 36.4 us
  Pallas kernels  35.6 us (98%)
  local copies, waits for them, and re-layouts  0.8 us (2%)
    pallas_call x1, Pallas kernels, on_device(): pl.pallas_call(functools.partial(kernel, layers, line, first, groups), ou...  35.6 us
    unnamed x1, local copies, waits for them, and re-layouts  0.8 us

profile of v5, /device:TPU:0, one launch (start us, length us, event | category | flops | bytes accessed | tf_op | source)
XLA Modules:
  0.0 36.4 jit_solution(14121289374731731616)
XLA Ops:
  0.0 35.6 %shard_map.55 = f32[64,2048]{1,0:T(8,128)S(1)} custom-call(bf16[2,2048,256]{2,1,0:T(8,128)(2,1)} %train_a.1, bf16[2,2048,256]{2,1,0:T(8,128)(2,1)} %train_g.1, bf16[2,128,256]{2,1,0:T(8,128)(2,1)} %test_a.1, bf16[2,128,256]{2,1,0:T(8,128)(2,1)} %test_g.1, s32[16,1,128]{2,1,0:T(1,128)} %bitcast.1), custom_call_target="tpu_custom_call" | custom-call | tf_op jit(solution)/shard_map/pallas_call | solution.py:452
  35.6 0.8 %copy.7 = f32[64,2048]{1,0:T(8,128)} copy(f32[64,2048]{1,0:T(8,128)S(1)} %shard_map.55) | data formatting | bytes 1048576

commit v6 on v5

--- a/solution.py
+++ b/solution.py
@@ -276,7 +276,7 @@
         return pltpu.make_async_remote_copy(
             src_ref=buf.at[here] if src is None else src,
             dst_ref=buf.at[here],
-            send_sem=send_sem.at[routes.index(route)],
+            send_sem=send_sem.at[axis[route] // 2],
             recv_sem=recv_sem.at[group_there(at, route, chunk)],
             device_id={"tok": partner[route]},
             device_id_type=MESH,
@@ -408,8 +408,8 @@
         for group in groups[at]:
             for _, _, out in group:
                 sent += out
-        for i, route in enumerate(routes):
-            total = sum(r == route for r, _ in sent)
+        for i in range(2):
+            total = sum(axis[route] // 2 == i for route, _ in sent)
             if total > 0:
                 all_of_them = buf.at[pl.ds(0, total)]
                 pltpu.make_async_remote_copy(
@@ -465,7 +465,7 @@
             dma((2,)),
             dma((1,)),
             dma((max(len(g) for g in groups),)),
-            dma((4,)),
+            dma((2,)),
             pltpu.SemaphoreType.REGULAR((4,)),
             dma((layers - 1, tiles)),
             dma((layers - 1, tiles)),

time: 36.5 us -> 36.5 us (level)
  no operation moved by 1% of the time
where the time goes in v6:
time: 36.5 us; the launch traced here: 36.3 us
  Pallas kernels  35.5 us (97%)
  local copies, waits for them, and re-layouts  0.8 us (2%)
    pallas_call x1, Pallas kernels, on_device(): pl.pallas_call(functools.partial(kernel, layers, line, first, groups), ou...  35.5 us
    unnamed x1, local copies, waits for them, and re-layouts  0.8 us

profile of v6, /device:TPU:0, one launch (start us, length us, event | category | flops | bytes accessed | tf_op | source)
XLA Modules:
  0.0 36.3 jit_solution(3088936392005052151)
XLA Ops:
  0.0 35.5 %shard_map.55 = f32[64,2048]{1,0:T(8,128)S(1)} custom-call(bf16[2,2048,256]{2,1,0:T(8,128)(2,1)} %train_a.1, bf16[2,2048,256]{2,1,0:T(8,128)(2,1)} %train_g.1, bf16[2,128,256]{2,1,0:T(8,128)(2,1)} %test_a.1, bf16[2,128,256]{2,1,0:T(8,128)(2,1)} %test_g.1, s32[16,1,128]{2,1,0:T(1,128)} %bitcast.1), custom_call_target="tpu_custom_call" | custom-call | tf_op jit(solution)/shard_map/pallas_call | solution.py:452
  35.5 0.8 %copy.7 = f32[64,2048]{1,0:T(8,128)} copy(f32[64,2048]{1,0:T(8,128)S(1)} %shard_map.55) | data formatting | bytes 1048576

commit v7 on v6

--- a/solution.py
+++ b/solution.py
@@ -312,6 +312,7 @@
         for route in used:
             pl.when(jnp.logical_not(lower[route]))(functools.partial(answered, route))
 
+    pl.when(core > 0)(lambda: pl.delay(500))
     branch(role, 0, roles, send_own)
 
     for which, src in enumerate((train_a, train_g)):

time: 36.5 us -> 36.4 us (level)
  no operation moved by 1% of the time
where the time goes in v7:
time: 36.4 us; the launch traced here: 36.2 us
  Pallas kernels  35.4 us (97%)
  local copies, waits for them, and re-layouts  0.8 us (2%)
    pallas_call x1, Pallas kernels, on_device(): pl.pallas_call(functools.partial(kernel, layers, line, first, groups), ou...  35.4 us
    unnamed x1, local copies, waits for them, and re-layouts  0.8 us

profile of v7, /device:TPU:0, one launch (start us, length us, event | category | flops | bytes accessed | tf_op | source)
XLA Modules:
  0.0 36.2 jit_solution(13401295503774465536)
XLA Ops:
  0.0 35.4 %shard_map.55 = f32[64,2048]{1,0:T(8,128)S(1)} custom-call(bf16[2,2048,256]{2,1,0:T(8,128)(2,1)} %train_a.1, bf16[2,2048,256]{2,1,0:T(8,128)(2,1)} %train_g.1, bf16[2,128,256]{2,1,0:T(8,128)(2,1)} %test_a.1, bf16[2,128,256]{2,1,0:T(8,128)(2,1)} %test_g.1, s32[16,1,128]{2,1,0:T(1,128)} %bitcast.1), custom_call_target="tpu_custom_call" | custom-call | tf_op jit(solution)/shard_map/pallas_call | solution.py:453
  35.4 0.8 %copy.7 = f32[64,2048]{1,0:T(8,128)} copy(f32[64,2048]{1,0:T(8,128)S(1)} %shard_map.55) | data formatting | bytes 1048576
